TPU v7x, 32 devices: a whole 2x2x4 slice. The times are simulated.
32 devices in a mesh: groups: 2 (over y), row: 4 (over z), col: 2 (over x), sub: 2 (over core).
Axes of the slice: x: 2, y: 2, z: 4, core: 2. Of those that a mesh axis runs over, the one named last changes fastest.
Arguments:
- query_acts: bfloat16 [64, 128, 4096], P(('groups', 'col', 'sub'), None, 'row'), parts along dimension 0, may hold values from -6 to 6
- query_grads: bfloat16 [64, 128, 4096], P(('groups', 'col', 'sub'), None, 'row'), parts along dimension 0, may hold values from -0.5390625 to 0.5390625
- proj_in: bfloat16 [4096, 128], P('row'), may hold values from -0.09375 to 0.09375
- proj_out: bfloat16 [4096, 128], P('row'), may hold values from -0.09375 to 0.09375
- inverse_gram: float32 [16384, 16384], P('row', ('col', 'sub')), may hold values from -0.01 to 2.01, as said below
- store_slab: bfloat16 [2048, 16384], P(('groups', 'col'), ('row', 'sub')), parts along dimension 0, may hold values from -0.046875 to 0.046875
Outputs:
- scores: float32 [64, 1024], P('groups', 'col'), parts along dimension 0
There are 2 independent parts, one for each index of `groups`. A program takes and returns all parts, laid end to end along the dimension named above; an argument that names none is the same for every part. Nothing has to cross between parts.
Inputs may be any that keep to these rules, and one draw needn't show every extreme that they name: inverse_gram is symmetric.
All inputs are finite; a program needn't handle non-finite values.
Results may differ from a plain program's by a relative error of at most 0.0029.
Values may be sent and summed in bfloat16 or wider, within the bound.
A program may use at most 128 MiB of HBM per device.

v0:
```python
import jax
import jax.numpy as jnp
from jax import lax
from jax.sharding import PartitionSpec as P


def body(query_acts, query_grads, proj_in, proj_out, inverse_gram, store_slab):
    row_count = lax.axis_size("row")
    row_index = lax.axis_index("row")
    sub_index = lax.axis_index("sub")
    in_width = proj_in.shape[1]
    act_part = jnp.einsum("qtd,dk->qtk", query_acts, proj_in, preferred_element_type=jnp.float32)
    grad_part = jnp.einsum("qtd,dk->qtk", query_grads, proj_out, preferred_element_type=jnp.float32)
    store_width = store_slab.shape[1]
    row_block = in_width // row_count
    act_whole, grad_proj = lax.psum((act_part, grad_part), "row")
    act_proj = lax.dynamic_slice_in_dim(act_whole, row_index * row_block, row_block, 2)
    kron_part = jnp.einsum("qta,qtb->qab", act_proj, grad_proj, precision=lax.Precision.HIGHEST)
    kron_feats = lax.all_gather(kron_part, ("col", "sub"), axis=0, tiled=True)
    features_flat = kron_feats.reshape(kron_feats.shape[0], -1)
    precond_part = jnp.dot(features_flat, inverse_gram, precision=lax.Precision.HIGHEST)
    precond_block = lax.psum(precond_part, "row").astype(jnp.bfloat16)
    precond_full = lax.all_gather(precond_block, ("col", "sub"), axis=1, tiled=True)
    store_start = (row_index * lax.axis_size("sub") + sub_index) * store_width
    precond_mine = lax.dynamic_slice_in_dim(precond_full, store_start, store_width, 1)
    score_part = lax.dot_general(
        precond_mine, store_slab, (((1,), (1,)), ((), ())), preferred_element_type=jnp.float32
    )
    return lax.psum(score_part, ("row", "sub"))


def solution(mesh):
    return jax.shard_map(
        body,
        mesh=mesh,
        in_specs=(
            P(("groups", "col", "sub"), None, "row"),
            P(("groups", "col", "sub"), None, "row"),
            P("row", None),
            P("row", None),
            P("row", ("col", "sub")),
            P(("groups", "col"), ("row", "sub")),
        ),
        out_specs=P("groups", "col"),
        check_vma=False,
    )
```

profile of v0, /device:TPU:0, one launch (start us, length us, event | category | flops | bytes accessed | tf_op | source)
XLA Modules:
  0.0 229.8 jit_solution(5424113497208901070)
XLA Ops:
  6.5 0.0 copy-start
  6.5 0.0 copy-start.2
  6.5 0.0 all-reduce.7.cloned.1.call-start
  6.5 1.6 copy-done
  8.1 0.0 copy-start.1
  8.1 2.6 %fusion.3 = f32[8,128,128]{2,1,0:T(8,128)} fusion(bf16[8,128,1024]{2,1,0:T(8,128)(2,1)S(1)} %copy-done, bf16[1024,128]{1,0:T(8,128)(2,1)} %param.9), kind=kOutput, calls=%fused_computation.3 | convolution fusion | flops 268435456 | bytes 2883584 | tf_op jit(solution)/shard_map/qtd,dk->qtk/dot_general | solution.py:13
  10.7 0.0 copy-done.2
  10.7 0.0 copy-done.1
  10.7 1.6 fusion.5
  12.4 0.0 all-reduce.7.cloned.1.call-update
  12.4 0.0 all-gather.2.cloned.1.call-start
  12.4 54.8 %all-reduce.7.cloned.1.call-done = (f32[8,128,128]{2,1,0:T(8,128)}, f32[8,128,128]{1,2,0:T(8,128)}) async-done(((f32[8,128,128]{2,1,0:T(8,128)}, f32[8,128,128]{1,2,0:T(8,128)}), (f32[8,128,128]{2,1,0:T(8,128)}, f32[8,128,128]{1,2,0:T(8,128)})) %all-reduce.7.cloned.1.call-update) | async-done | bytes 1048592 | tf_op jit(solution)/shard_map/psum | solution.py:16
  67.2 1.7 fusion.9
  68.9 7.1 %all_gather.6 = f32[32,32,128]{2,1,0:T(8,128)S(1)} all-gather(f32[8,32,128]{2,1,0:T(8,128)S(1)} %fusion.9), channel_id=1, replica_groups=mesh['groups'=2,'row'=4,'col'=2,'sub'=2] {'col','sub'}, dimensions={0}, use_global_device_ids=true | all-gather | bytes 655360 | tf_op jit(solution)/shard_map/all_gather | solution.py:19
  76.0 43.6 %fusion = f32[32,4096]{1,0:T(8,128)S(1)} fusion(f32[4096,4096]{1,0:T(8,128)} %param.10, f32[4,8,32,128]{3,2,1,0:T(8,128)S(1)} %bitcast.15), kind=kOutput, calls=%fused_computation | convolution fusion | flops 6442450944 | bytes 68157440 | tf_op jit(solution)/shard_map/dot_general | solution.py:21
  119.6 29.2 %all-reduce.8 = bf16[32,4096]{1,0:T(8,128)(2,1)} all-reduce(f32[32,4096]{1,0:T(8,128)S(1)} %fusion), channel_id=1, replica_groups=mesh['groups'=2,'row'=4,'col'=2,'sub'=2] {'row'}, use_global_device_ids=true, to_apply=%region_2.0 | all-reduce | flops 131072 | bytes 786432 | tf_op jit(solution)/shard_map/psum | solution.py:22
  148.8 0.0 all-gather.2.cloned.1.call-update
  148.8 0.0 all-reduce.5.cloned.1.call-start
  148.9 15.0 %all-gather.2.cloned.1.call-done = bf16[32,16384]{1,0:T(8,128)(2,1)} async-done(((bf16[32,4096]{1,0:T(8,128)(2,1)}), bf16[32,16384]{1,0:T(8,128)(2,1)}) %all-gather.2.cloned.1.call-update) | async-done | bytes 1048592 | tf_op jit(solution)/shard_map/all_gather | solution.py:23
  163.9 3.0 %fusion.7 = f32[32,512]{1,0:T(8,128)} fusion(bf16[512,2048]{1,0:T(8,128)(2,1)} %param.11, bf16[32,16384]{1,0:T(8,128)(2,1)} %all-gather.2.cloned.1.call-done, s32[]{:T(128)S(6)} %select_n.7), kind=kOutput, calls=%fused_computation.7 | convolution fusion | flops 67108864 | bytes 2293764 | tf_op jit(solution)/shard_map/dot_general | solution.py:26
  166.9 0.0 all-reduce.5.cloned.1.call-update
  166.9 54.9 %all-reduce.5.cloned.1.call-done = f32[32,512]{1,0:T(8,128)} async-done(((f32[32,512]{1,0:T(8,128)}), f32[32,512]{1,0:T(8,128)}) %all-reduce.5.cloned.1.call-update) | async-done | bytes 65552 | tf_op jit(solution)/shard_map/psum | solution.py:29
  221.8 1.5 copy.17
Async XLA Ops:
  6.5 1.6 copy-start
  6.5 4.2 %copy-start.2 = (bf16[1024,128]{1,0:T(8,128)(2,1)S(1)}, bf16[1024,128]{1,0:T(8,128)(2,1)}, u32[]{:S(2)}) copy-start(bf16[1024,128]{1,0:T(8,128)(2,1)} %param.8) | copy-start | bytes 786436
  6.5 60.7 %all-reduce.7.cloned.1.call-start = ((), (), s32[]{:S(2)}) async-start(), calls=%async_computation.2 | async-start | bytes 2097152 | tf_op jit(solution)/shard_map/psum | solution.py:16
  8.1 2.6 %copy-start.1 = (bf16[8,128,1024]{2,1,0:T(8,128)(2,1)S(1)}, bf16[8,128,1024]{2,1,0:T(8,128)(2,1)}, u32[]{:S(2)}) copy-start(bf16[8,128,1024]{2,1,0:T(8,128)(2,1)} %param.6) | copy-start | bytes 6291460
  12.4 151.5 %all-gather.2.cloned.1.call-start = ((), (), s32[]{:S(2)}) async-start(), calls=%async_computation | async-start | bytes 1310720 | tf_op jit(solution)/shard_map/all_gather | solution.py:23
  148.8 73.0 %all-reduce.5.cloned.1.call-start = ((), (), s32[]{:S(2)}) async-start(), calls=%async_computation.1 | async-start | bytes 131072 | tf_op jit(solution)/shard_map/psum | solution.py:29
Sparse Core Ops, SparseCore 0:
  12.5 54.6 all-reduce.6
  148.9 14.9 all-gather.1
  167.1 54.6 all-reduce.4
where the time goes:
time: 230 us
  waiting for transfers between devices  125 us (54%)
  matrix products  52.5 us (23%)
  blocking collectives  36.3 us (16%)
  between operations  13.1 us (6%)
  local copies, waits for them, and re-layouts  3.07 us (1%)
    psum x1, waiting for transfers between devices, body(): return lax.psum(score_part, ('row', 'sub'))  54.9 us
    psum x1, waiting for transfers between devices, body(): act_whole, grad_proj = lax.psum((act_part, grad_part), 'row')  54.8 us
    dot_general x1, matrix products, body(): jnp.dot(features_flat, inverse_gram, precision=lax.Precision.HIGHEST)  43.6 us
    psum x1, blocking collectives, body(): precond_block = lax.psum(precond_part, 'row').astype(jnp.bfloat16)  29.2 us
    all_gather x1, waiting for transfers between devices, body(): lax.all_gather(precond_block, ('col', 'sub'), axis=1, tiled=True)  15 us
    all_gather x1, blocking collectives, body(): kron_feats = lax.all_gather(kron_part, ('col', 'sub'), axis=0, tiled=True)  7.14 us
  transfers between devices with their start and end apart: 3, of which 3 were waited for; matrix products, arithmetic and copies ran while one was open for 0% of the time, Pallas kernels for 0%

commit v1 on v0

v1 whole, which is shorter than its diff:
```python
import functools

import jax
import jax.numpy as jnp
from jax import lax
from jax.experimental import pallas as pl
from jax.experimental.pallas import tpu as pltpu
from jax.sharding import PartitionSpec as P

F32, BF16 = jnp.float32, jnp.bfloat16
SLOTS = 9


def split(x):
    hi = x.astype(BF16)
    return hi, (x - hi.astype(F32)).astype(BF16)


def kernel(rows, cols, subs, acts_h, grads_h, pin_h, pout_h, gram_h, store_h, out,
           acts, grads, pin, pout, gram, store, part, recv, feats, fbuf, ft, pt, pre, sub_in, col_in,
           own, own_s, half_in, half_all, half_out,
           in_sem, gram_sem, rs_send, rs_recv, fx_send, fx_recv, fx_local, fz_send, fz_recv,
           ps_sem, pc_send, pc_recv, ss_sem, sz_send, sz_recv, sl_sem, sf_sem):
    g, r, c, s = (lax.axis_index(n) for n in ("groups", "row", "col", "sub"))
    queries = acts.shape[0]
    half = queries // 2
    planes = cols * subs
    me = c * subs + s
    aw = fbuf.shape[2]
    mb, kb = gram.shape[1], gram.shape[2]
    grows, gcols = gram_h.shape
    nk, ni = gcols // kb, grows // mb
    blocks = nk * ni

    def dev(row, col, sub):
        return {"groups": g, "row": row, "col": col, "sub": sub}

    def remote(src, dst, send, rcv, row, col, sub):
        return pltpu.make_async_remote_copy(
            src_ref=src, dst_ref=dst, send_sem=send, recv_sem=rcv,
            device_id=dev(row, col, sub), device_id_type=pl.DeviceIdType.MESH)

    loads = [pltpu.make_async_copy(a, b, in_sem.at[i]) for i, (a, b) in enumerate(
        ((pin_h, pin), (pout_h, pout), (acts_h, acts), (grads_h, grads), (store_h, store)))]
    for l in loads[:4]:
        l.start()

    def gram_copy(b):
        k, i = b // ni, b % ni
        slot = lax.rem(b, SLOTS)
        return pltpu.make_async_copy(
            gram_h.at[pl.ds(pl.multiple_of(i * mb, mb), mb), pl.ds(pl.multiple_of(k * kb, kb), kb)],
            gram.at[slot], gram_sem.at[slot])

    for b in range(min(SLOTS, blocks)):
        gram_copy(b).start()
    loads[4].start()

    barrier = pltpu.get_barrier_semaphore()
    count = 0
    for d in range(1, rows):
        pl.semaphore_signal(barrier, inc=1, device_id=dev(lax.rem(r + d, rows), c, s), device_id_type=pl.DeviceIdType.MESH)
        count += 1
    for d in range(1, planes):
        o = lax.rem(me + d, planes)
        pl.semaphore_signal(barrier, inc=1, device_id=dev(r, o // subs, lax.rem(o, subs)), device_id_type=pl.DeviceIdType.MESH)
        count += 1

    def project(q):
        part[q, 0] = jnp.dot(acts[q], pin[...], preferred_element_type=F32)
        part[q, 1] = jnp.dot(grads[q], pout[...], preferred_element_type=F32)

    for l in loads[:4]:
        l.wait()
    for q in range(queries):
        project(q)
    pl.semaphore_wait(barrier, count)

    starts = (r == 0, r == rows - 1)
    ends = (r == rows - 1, r == 0)
    ahead = (jnp.minimum(r + 1, rows - 1), jnp.maximum(r - 1, 0))
    behind = (jnp.maximum(r - 1, 0), jnp.minimum(r + 1, rows - 1))

    def rs_copy(h, q, w):
        return remote(part.at[q, w], recv.at[q, w], rs_send.at[q, w], rs_recv.at[q, w], ahead[h], c, s)

    def fx_copy(q, d):
        o = lax.rem(me + d, planes)
        return remote(feats.at[lax.rem(q, half), pl.ds(pl.multiple_of(o * aw, aw), aw)], fbuf.at[me, q],
                      fx_send.at[lax.rem(q, half), d], fx_recv.at[lax.rem(q, half), d], r, o // subs, lax.rem(o, subs))

    def fx_own(q):
        return pltpu.make_async_copy(feats.at[lax.rem(q, half), pl.ds(pl.multiple_of(me * aw, aw), aw)],
                                     fbuf.at[me, q], fx_local.at[lax.rem(q, half)])

    def fz_copy(h, q):
        return remote(fbuf.at[:, q], fbuf.at[:, q], fz_send.at[q], fz_recv.at[q], behind[h], c, s)

    def send_row(h, q):
        for d in range(1, planes):
            fx_copy(q, d).wait()
        fx_own(q).wait()
        fz_copy(h, q).start()

    for k in range(half):
        for w in range(2):
            for h in range(2):
                q = h * half + k

                @pl.when(jnp.logical_not(starts[h]))
                def _():
                    rs_copy(h, q, w).wait_recv()
                    part[q, w] = part[q, w] + recv[q, w]

                @pl.when(jnp.logical_not(ends[h]))
                def _():
                    rs_copy(h, q, w).start()
        for h in range(2):
            q = h * half + k

            @pl.when(ends[h])
            def _():
                feats[k] = jnp.dot(part[q, 0].T, part[q, 1], precision=lax.Precision.HIGHEST,
                                   preferred_element_type=F32)
                for d in range(1, planes):
                    fx_copy(q, d).start()
                fx_own(q).start()
                if k:
                    send_row(h, q - 1)
    for h in range(2):
        @pl.when(ends[h])
        def _():
            send_row(h, h * half + half - 1)

    for k in range(half):
        for h in range(2):
            q = h * half + k

            @pl.when(jnp.logical_not(ends[h]))
            def _():
                fz_copy(h, q).wait_recv()

            @pl.when(jnp.logical_not(jnp.logical_or(starts[h], ends[h])))
            def _():
                fz_copy(h, q).start()
    for k in range(half):
        for h in range(2):
            q = h * half + k

            @pl.when(jnp.logical_not(starts[h]))
            def _():
                fz_copy(h, q).wait_send()

            @pl.when(jnp.logical_not(ends[h]))
            def _():
                for w in range(2):
                    rs_copy(h, q, w).wait_send()

    nq = planes * queries
    width = ft.shape[1]
    for a in range(aw):
        x = fbuf[:, :, a, :].reshape(nq, fbuf.shape[3])
        hi, lo = split(x)
        hi, lo = hi.astype(F32), lo.astype(F32)
        rest = [jnp.zeros((width - 2 * nq, x.shape[1]), F32)] if width > 2 * nq else []
        y = jnp.concatenate([hi, lo] + rest, axis=0)
        ft[a * x.shape[1]:(a + 1) * x.shape[1], :] = y.T.astype(BF16)

    step = min(256, mb)

    def block(b, _):
        k, i = b // ni, b % ni
        slot = lax.rem(b, SLOTS)
        gram_copy(b).wait()
        w = ft[pl.ds(pl.multiple_of(k * kb, kb), kb), :]

        def inner(m, _):
            rows_at = pl.multiple_of(m * step, step)
            hi, lo = split(gram[slot, pl.ds(rows_at, step), :])
            acc = jnp.dot(hi, w, preferred_element_type=F32) + jnp.dot(lo, w, preferred_element_type=F32)
            at = pl.ds(pl.multiple_of(i * mb + m * step, step), step)

            @pl.when(k == 0)
            def _():
                pt[at, :] = acc

            @pl.when(k > 0)
            def _():
                pt[at, :] = pt[at, :] + acc
            return 0

        lax.fori_loop(0, mb // step, inner, 0)

        @pl.when(b + SLOTS < blocks)
        def _():
            gram_copy(b + SLOTS).start()
        return 0

    lax.fori_loop(0, blocks, block, 0)

    tile = 128
    for j in range(grows // tile):
        t = pt[j * tile:(j + 1) * tile, :].T
        per = pre.shape[2] // tile
        pre[j // per, :, (j % per) * tile:(j % per + 1) * tile] = t[:nq] + t[nq:2 * nq]
    other = lax.rem(s + 1, subs)
    x_sub = remote(pre.at[other], sub_in, ps_sem.at[0], ps_sem.at[1], r, c, other)
    x_sub.start()
    x_sub.wait()
    pre[s] = pre[s] + sub_in[...]
    x_cols = [remote(pre.at[s], col_in.at[c], pc_send.at[d], pc_recv.at[d], r, lax.rem(c + d, cols), s)
              for d in range(1, cols)]
    for x in x_cols:
        x.start()
    col_in[c] = pre[s]
    for x in x_cols:
        x.wait()
    total = col_in[0]
    for o in range(1, cols):
        total = total + col_in[o]
    loads[4].wait()
    score = lax.dot_general(total.astype(BF16), store[...], (((1,), (1,)), ((), ())), preferred_element_type=F32)

    hq = nq // subs
    for o in range(subs):
        own[o] = score[o * hq:(o + 1) * hq]
    x_half = remote(own.at[other], half_in, ss_sem.at[0], ss_sem.at[1], r, c, other)
    x_half.start()
    x_half.wait()
    own_s[...] = own[s] + half_in[...]
    x_rows = [remote(own_s, half_all.at[r], sz_send.at[d], sz_recv.at[d], lax.rem(r + d, rows), c, s)
              for d in range(1, rows)]
    for x in x_rows:
        x.start()
    half_all[r] = own_s[...]
    for x in x_rows:
        x.wait()
    total = half_all[0]
    for o in range(1, rows):
        total = total + half_all[o]
    half_out[s] = total
    x_out = remote(half_out.at[s], half_out.at[s], sf_sem.at[0], sf_sem.at[1], r, c, other)
    x_out.start()
    x_out.wait()
    for o in range(subs):
        out[o * hq:(o + 1) * hq, :] = half_out[o]


def body(sizes, query_acts, query_grads, proj_in, proj_out, inverse_gram, store_slab):
    rows, cols, subs = sizes
    queries, tokens, depth = query_acts.shape
    kin, kout = proj_in.shape[1], proj_out.shape[1]
    planes = cols * subs
    nq = planes * queries
    aw = kin // planes
    grows, gcols = inverse_gram.shape
    mb, kb = min(512, grows), min(2048, gcols)
    examples, width = store_slab.shape
    half = queries // 2
    hq = nq // subs
    dma = pltpu.SemaphoreType.DMA
    lanes = -(-2 * nq // 128) * 128
    scratch = [
        pltpu.VMEM(query_acts.shape, BF16), pltpu.VMEM(query_grads.shape, BF16),
        pltpu.VMEM(proj_in.shape, BF16), pltpu.VMEM(proj_out.shape, BF16),
        pltpu.VMEM((SLOTS, mb, kb), F32), pltpu.VMEM(store_slab.shape, BF16),
        pltpu.VMEM((queries, 2, tokens, kin), F32), pltpu.VMEM((queries, 2, tokens, kin), F32),
        pltpu.VMEM((half, kin, kout), F32), pltpu.VMEM((planes, queries, aw, kout), F32),
        pltpu.VMEM((gcols, lanes), BF16), pltpu.VMEM((grows, lanes), F32),
        pltpu.VMEM((subs, nq, width), F32), pltpu.VMEM((nq, width), F32), pltpu.VMEM((cols, nq, width), F32),
        pltpu.VMEM((subs, hq, examples), F32), pltpu.VMEM((hq, examples), F32), pltpu.VMEM((hq, examples), F32),
        pltpu.VMEM((rows, hq, examples), F32), pltpu.VMEM((subs, hq, examples), F32),
        dma((5,)), dma((SLOTS,)), dma((queries, 2)), dma((queries, 2)),
        dma((half, planes)), dma((half, planes)), dma((half,)), dma((queries,)), dma((queries,)),
        dma((2,)), dma((cols,)), dma((cols,)), dma((2,)), dma((rows,)), dma((rows,)), dma((1,)), dma((2,)),
    ]
    return pl.pallas_call(
        functools.partial(kernel, rows, cols, subs),
        out_shape=jax.ShapeDtypeStruct((nq, examples), F32),
        in_specs=[pl.BlockSpec(memory_space=pltpu.HBM)] * 6,
        out_specs=pl.BlockSpec(memory_space=pltpu.VMEM),
        scratch_shapes=scratch,
        compiler_params=pltpu.CompilerParams(
            collective_id=0, has_side_effects=True, vmem_limit_bytes=67043328),
        name="influence",
    )(query_acts, query_grads, proj_in, proj_out, inverse_gram, store_slab)


def solution(mesh):
    sizes = (mesh.shape["row"], mesh.shape["col"], mesh.shape["sub"])
    return jax.shard_map(
        functools.partial(body, sizes),
        mesh=mesh,
        in_specs=(
            P(("groups", "col", "sub"), None, "row"),
            P(("groups", "col", "sub"), None, "row"),
            P("row", None),
            P("row", None),
            P("row", ("col", "sub")),
            P(("groups", "col"), ("row", "sub")),
        ),
        out_specs=P("groups", "col"),
        check_vma=False,
    )
```

time: 230 us -> 244 us (1.061)
  Pallas kernels: 0 us -> 243 us
  waiting for transfers between devices: 125 us -> 0 us
  matrix products: 52.5 us -> 0 us
  blocking collectives: 36.3 us -> 0 us
  between operations: 13.1 us -> 0.01 us
    pallas_call x0 -> x1, Pallas kernels: none -> 243 us  [body(): pl.pallas_call(functools.partial(kernel, rows, cols, subs), out_shape=jax...]
    psum x2 -> x0, waiting for transfers between devices: 110 us -> none  [the longest x1 54.9 us: body(): return lax.psum(score_part, ('row', 'sub'))]
    dot_general x5 -> x0, matrix products: 52.5 us -> none  [the longest x1 43.6 us: body(): jnp.dot(features_flat, inverse_gram, precision=lax.Precision.HIGHEST)]
    psum x1 -> x0, blocking collectives: 29.2 us -> none  [body(): precond_block = lax.psum(precond_part, 'row').astype(jnp.bfloat16)]
    all_gather x1 -> x0, waiting for transfers between devices: 15 us -> none  [body(): lax.all_gather(precond_block, ('col', 'sub'), axis=1, tiled=True)]
    all_gather x1 -> x0, blocking collectives: 7.14 us -> none  [body(): kron_feats = lax.all_gather(kron_part, ('col', 'sub'), axis=0, tiled=True)]
  transfers between devices with their start and end apart: 3 -> 0, of which waited for: 3 -> 0; matrix products, arithmetic and copies ran while one was open for 0% -> 0% of each run, Pallas kernels for 0% -> 0%
where the time goes in v1:
time: 244 us
  Pallas kernels  243 us (100%)
    pallas_call x1, Pallas kernels, body(): pl.pallas_call(functools.partial(kernel, rows, cols, subs), out_shape=jax...  243 us

profile of v1, /device:TPU:0, one launch (start us, length us, event | category | flops | bytes accessed | tf_op | source)
XLA Modules:
  0.0 244.2 jit_solution(6535034414044702966)
XLA Ops:
  0.0 242.7 %influence.1 = f32[32,512]{1,0:T(8,128)} custom-call(bf16[8,128,1024]{2,1,0:T(8,128)(2,1)} %acts_h.1, bf16[8,128,1024]{2,1,0:T(8,128)(2,1)} %grads_h.1, bf16[1024,128]{1,0:T(8,128)(2,1)} %pin_h.1, bf16[1024,128]{1,0:T(8,128)(2,1)} %pout_h.1, f32[4096,4096]{1,0:T(8,128)} %gram_h.1, bf16[512,2048]{1,0:T(8,128)(2,1)} %store_h.1), custom_call_target="tpu_custom_call" | custom-call | tf_op jit(solution)/shard_map/influence/pallas_call | solution.py:277
  242.8 1.5 copy.8

commit v2 on v1

--- a/solution.py
+++ b/solution.py
@@ -102,47 +102,57 @@
         fx_own(q).wait()
         fz_copy(h, q).start()
 
-    for k in range(half):
-        for w in range(2):
-            for h in range(2):
-                q = h * half + k
-
-                @pl.when(jnp.logical_not(starts[h]))
-                def _():
-                    rs_copy(h, q, w).wait_recv()
-                    part[q, w] = part[q, w] + recv[q, w]
-
-                @pl.when(jnp.logical_not(ends[h]))
-                def _():
-                    rs_copy(h, q, w).start()
+    def sums(t, _):
         for h in range(2):
+            j = t - (r if h == 0 else rows - 1 - r)
+            k, w = j // 2, lax.rem(j, 2)
             q = h * half + k
-
-            @pl.when(ends[h])
+            live = jnp.logical_and(j >= 0, j < 2 * half)
+
+            @pl.when(jnp.logical_and(live, jnp.logical_not(starts[h])))
+            def _():
+                rs_copy(h, q, w).wait_recv()
+                part[q, w] = part[q, w] + recv[q, w]
+
+            @pl.when(jnp.logical_and(live, jnp.logical_not(ends[h])))
+            def _():
+                rs_copy(h, q, w).start()
+
+            @pl.when(jnp.logical_and(jnp.logical_and(live, ends[h]), w == 1))
             def _():
                 feats[k] = jnp.dot(part[q, 0].T, part[q, 1], precision=lax.Precision.HIGHEST,
                                    preferred_element_type=F32)
                 for d in range(1, planes):
                     fx_copy(q, d).start()
                 fx_own(q).start()
-                if k:
+
+                @pl.when(k > 0)
+                def _():
                     send_row(h, q - 1)
+        return 0
+
+    lax.fori_loop(0, 2 * half + rows - 1, sums, 0)
     for h in range(2):
         @pl.when(ends[h])
         def _():
             send_row(h, h * half + half - 1)
 
-    for k in range(half):
+    def back(t, _):
         for h in range(2):
+            k = t - (rows - 1 - r if h == 0 else r)
             q = h * half + k
-
-            @pl.when(jnp.logical_not(ends[h]))
+            live = jnp.logical_and(k >= 0, k < half)
+
+            @pl.when(jnp.logical_and(live, jnp.logical_not(ends[h])))
             def _():
                 fz_copy(h, q).wait_recv()
 
-            @pl.when(jnp.logical_not(jnp.logical_or(starts[h], ends[h])))
+            @pl.when(jnp.logical_and(live, jnp.logical_not(jnp.logical_or(starts[h], ends[h]))))
             def _():
                 fz_copy(h, q).start()
+        return 0
+
+    lax.fori_loop(0, half + rows - 1, back, 0)
     for k in range(half):
         for h in range(2):
             q = h * half + k

time: 244 us -> 105 us (0.43)
  Pallas kernels: 243 us -> 103 us
    pallas_call x1, Pallas kernels: 243 us -> 103 us  [body(): pl.pallas_call(functools.partial(kernel, rows, cols, subs), out_shape=jax...]
where the time goes in v2:
time: 105 us
  Pallas kernels  103 us (98%)
  local copies, waits for them, and re-layouts  1.47 us (1%)
    pallas_call x1, Pallas kernels, body(): pl.pallas_call(functools.partial(kernel, rows, cols, subs), out_shape=jax...  103 us

profile of v2, /device:TPU:0, one launch (start us, length us, event | category | flops | bytes accessed | tf_op | source)
XLA Modules:
  0.0 104.9 jit_solution(486928076442494256)
XLA Ops:
  0.0 103.4 %influence.1 = f32[32,512]{1,0:T(8,128)} custom-call(bf16[8,128,1024]{2,1,0:T(8,128)(2,1)} %acts_h.1, bf16[8,128,1024]{2,1,0:T(8,128)(2,1)} %grads_h.1, bf16[1024,128]{1,0:T(8,128)(2,1)} %pin_h.1, bf16[1024,128]{1,0:T(8,128)(2,1)} %pout_h.1, f32[4096,4096]{1,0:T(8,128)} %gram_h.1, bf16[512,2048]{1,0:T(8,128)(2,1)} %store_h.1), custom_call_target="tpu_custom_call" | custom-call | tf_op jit(solution)/shard_map/influence/pallas_call | solution.py:287
  103.4 1.5 %copy.8 = f32[32,512]{1,0:T(8,128)} copy(f32[32,512]{1,0:T(8,128)} %influence.1) | data formatting | bytes 131072

commit v3 on v2

--- a/solution.py
+++ b/solution.py
@@ -9,6 +9,7 @@
 
 F32, BF16 = jnp.float32, jnp.bfloat16
 SLOTS = 9
+LAG = 2
 
 
 def split(x):
@@ -104,7 +105,7 @@
 
     def sums(t, _):
         for h in range(2):
-            j = t - (r if h == 0 else rows - 1 - r)
+            j = t - LAG * (r if h == 0 else rows - 1 - r)
             k, w = j // 2, lax.rem(j, 2)
             q = h * half + k
             live = jnp.logical_and(j >= 0, j < 2 * half)
@@ -131,7 +132,7 @@
                     send_row(h, q - 1)
         return 0
 
-    lax.fori_loop(0, 2 * half + rows - 1, sums, 0)
+    lax.fori_loop(0, 2 * half + LAG * (rows - 1), sums, 0)
     for h in range(2):
         @pl.when(ends[h])
         def _():
@@ -139,7 +140,7 @@
 
     def back(t, _):
         for h in range(2):
-            k = t - (rows - 1 - r if h == 0 else r)
+            k = t - LAG * (rows - 1 - r if h == 0 else r)
             q = h * half + k
             live = jnp.logical_and(k >= 0, k < half)
 
@@ -152,7 +153,7 @@
                 fz_copy(h, q).start()
         return 0
 
-    lax.fori_loop(0, half + rows - 1, back, 0)
+    lax.fori_loop(0, half + LAG * (rows - 1), back, 0)
     for k in range(half):
         for h in range(2):
             q = h * half + k
@@ -186,8 +187,7 @@
 
         def inner(m, _):
             rows_at = pl.multiple_of(m * step, step)
-            hi, lo = split(gram[slot, pl.ds(rows_at, step), :])
-            acc = jnp.dot(hi, w, preferred_element_type=F32) + jnp.dot(lo, w, preferred_element_type=F32)
+            acc = jnp.dot(gram[slot, pl.ds(rows_at, step), :].astype(BF16), w, preferred_element_type=F32)
             at = pl.ds(pl.multiple_of(i * mb + m * step, step), step)
 
             @pl.when(k == 0)
@@ -229,7 +229,9 @@
     for o in range(1, cols):
         total = total + col_in[o]
     loads[4].wait()
-    score = lax.dot_general(total.astype(BF16), store[...], (((1,), (1,)), ((), ())), preferred_element_type=F32)
+    score = lax.dot_general(jnp.concatenate(split(total), axis=0), store[...], (((1,), (1,)), ((), ())),
+                            preferred_element_type=F32)
+    score = score[:nq] + score[nq:]
 
     hq = nq // subs
     for o in range(subs):

time: 105 us -> 84.1 us (0.80)
  Pallas kernels: 103 us -> 82.5 us
    pallas_call x1, Pallas kernels: 103 us -> 82.5 us  [body(): pl.pallas_call(functools.partial(kernel, rows, cols, subs), out_shape=jax...]
where the time goes in v3:
time: 84.1 us; the launch traced here: 83.9 us
  Pallas kernels  82.5 us (98%)
  local copies, waits for them, and re-layouts  1.47 us (2%)
    pallas_call x1, Pallas kernels, body(): pl.pallas_call(functools.partial(kernel, rows, cols, subs), out_shape=jax...  82.5 us

profile of v3, /device:TPU:0, one launch (start us, length us, event | category | flops | bytes accessed | tf_op | source)
XLA Modules:
  0.0 83.9 jit_solution(17923005470963192039)
XLA Ops:
  0.0 82.5 %influence.1 = f32[32,512]{1,0:T(8,128)} custom-call(bf16[8,128,1024]{2,1,0:T(8,128)(2,1)} %acts_h.1, bf16[8,128,1024]{2,1,0:T(8,128)(2,1)} %grads_h.1, bf16[1024,128]{1,0:T(8,128)(2,1)} %pin_h.1, bf16[1024,128]{1,0:T(8,128)(2,1)} %pout_h.1, f32[4096,4096]{1,0:T(8,128)} %gram_h.1, bf16[512,2048]{1,0:T(8,128)(2,1)} %store_h.1), custom_call_target="tpu_custom_call" | custom-call | tf_op jit(solution)/shard_map/influence/pallas_call | solution.py:289
  82.5 1.5 %copy.8 = f32[32,512]{1,0:T(8,128)} copy(f32[32,512]{1,0:T(8,128)} %influence.1) | data formatting | bytes 131072

commit v4 on v3

--- a/solution.py
+++ b/solution.py
@@ -8,7 +8,7 @@
 from jax.sharding import PartitionSpec as P
 
 F32, BF16 = jnp.float32, jnp.bfloat16
-SLOTS = 9
+SLOTS = 11
 LAG = 2
 
 
@@ -18,10 +18,10 @@
 
 
 def kernel(rows, cols, subs, acts_h, grads_h, pin_h, pout_h, gram_h, store_h, out,
-           acts, grads, pin, pout, gram, store, part, recv, feats, fbuf, ft, pt, pre, sub_in, col_in,
+           acts, grads, pin, pout, gram, store, part, recv, feats, fbuf, ft, pre, sub_in, col_in,
            own, own_s, half_in, half_all, half_out,
            in_sem, gram_sem, rs_send, rs_recv, fx_send, fx_recv, fx_local, fz_send, fz_recv,
-           ps_sem, pc_send, pc_recv, ss_sem, sz_send, sz_recv, sl_sem, sf_sem):
+           ps_send, ps_recv, pc_send, pc_recv, ss_sem, sz_send, sz_recv, sl_sem, sf_sem):
     g, r, c, s = (lax.axis_index(n) for n in ("groups", "row", "col", "sub"))
     queries = acts.shape[0]
     half = queries // 2
@@ -32,6 +32,8 @@
     grows, gcols = gram_h.shape
     nk, ni = gcols // kb, grows // mb
     blocks = nk * ni
+    per = ni // subs
+    other = lax.rem(s + 1, subs)
 
     def dev(row, col, sub):
         return {"groups": g, "row": row, "col": col, "sub": sub}
@@ -47,7 +49,8 @@
         l.start()
 
     def gram_copy(b):
-        k, i = b // ni, b % ni
+        n, k = b // nk, b % nk
+        i = lax.rem(other * per + n, ni)
         slot = lax.rem(b, SLOTS)
         return pltpu.make_async_copy(
             gram_h.at[pl.ds(pl.multiple_of(i * mb, mb), mb), pl.ds(pl.multiple_of(k * kb, kb), kb)],
@@ -179,58 +182,55 @@
 
     step = min(256, mb)
 
-    def block(b, _):
-        k, i = b // ni, b % ni
-        slot = lax.rem(b, SLOTS)
-        gram_copy(b).wait()
-        w = ft[pl.ds(pl.multiple_of(k * kb, kb), kb), :]
-
-        def inner(m, _):
-            rows_at = pl.multiple_of(m * step, step)
-            acc = jnp.dot(gram[slot, pl.ds(rows_at, step), :].astype(BF16), w, preferred_element_type=F32)
-            at = pl.ds(pl.multiple_of(i * mb + m * step, step), step)
-
-            @pl.when(k == 0)
-            def _():
-                pt[at, :] = acc
-
-            @pl.when(k > 0)
-            def _():
-                pt[at, :] = pt[at, :] + acc
-            return 0
-
-        lax.fori_loop(0, mb // step, inner, 0)
-
-        @pl.when(b + SLOTS < blocks)
+    def sub_copy(p):
+        return remote(pre.at[p], sub_in.at[p], ps_send.at[p], ps_recv.at[p], r, c, other)
+
+    def col_copy(p, d):
+        return remote(pre.at[per + p], col_in.at[c, p], pc_send.at[d, p], pc_recv.at[d, p], r, lax.rem(c + d, cols), s)
+
+    def block(n, _):
+        for k in range(nk):
+            gram_copy(n * nk + k).wait()
+        for m in range(mb // step):
+            acc = None
+            for k in range(nk):
+                slot = lax.rem(n * nk + k, SLOTS)
+                term = jnp.dot(gram[slot, m * step:(m + 1) * step, :].astype(BF16), ft[k * kb:(k + 1) * kb, :],
+                               preferred_element_type=F32)
+                acc = term if acc is None else acc + term
+            t = acc.T
+            pre[n, :, m * step:(m + 1) * step] = t[:nq] + t[nq:2 * nq]
+        for k in range(nk):
+            @pl.when(n * nk + k + SLOTS < blocks)
+            def _():
+                gram_copy(n * nk + k + SLOTS).start()
+
+        @pl.when(n < per)
         def _():
-            gram_copy(b + SLOTS).start()
+            sub_copy(n).start()
+
+        @pl.when(n >= per)
+        def _():
+            sub_copy(n - per).wait_recv()
+            pre[n] = pre[n] + sub_in[n - per]
+            for d in range(1, cols):
+                col_copy(n - per, d).start()
+            col_in[c, n - per] = pre[n]
         return 0
 
-    lax.fori_loop(0, blocks, block, 0)
-
-    tile = 128
-    for j in range(grows // tile):
-        t = pt[j * tile:(j + 1) * tile, :].T
-        per = pre.shape[2] // tile
-        pre[j // per, :, (j % per) * tile:(j % per + 1) * tile] = t[:nq] + t[nq:2 * nq]
-    other = lax.rem(s + 1, subs)
-    x_sub = remote(pre.at[other], sub_in, ps_sem.at[0], ps_sem.at[1], r, c, other)
-    x_sub.start()
-    x_sub.wait()
-    pre[s] = pre[s] + sub_in[...]
-    x_cols = [remote(pre.at[s], col_in.at[c], pc_send.at[d], pc_recv.at[d], r, lax.rem(c + d, cols), s)
-              for d in range(1, cols)]
-    for x in x_cols:
-        x.start()
-    col_in[c] = pre[s]
-    for x in x_cols:
-        x.wait()
-    total = col_in[0]
-    for o in range(1, cols):
-        total = total + col_in[o]
+    lax.fori_loop(0, ni, block, 0)
     loads[4].wait()
-    score = lax.dot_general(jnp.concatenate(split(total), axis=0), store[...], (((1,), (1,)), ((), ())),
-                            preferred_element_type=F32)
+    score = None
+    for p in range(per):
+        for d in range(1, cols):
+            col_copy(p, d).wait()
+        sub_copy(p).wait_send()
+        total = col_in[0, p]
+        for o in range(1, cols):
+            total = total + col_in[o, p]
+        term = lax.dot_general(jnp.concatenate(split(total), axis=0), store[:, p * mb:(p + 1) * mb],
+                               (((1,), (1,)), ((), ())), preferred_element_type=F32)
+        score = term if score is None else score + term
     score = score[:nq] + score[nq:]
 
     hq = nq // subs
@@ -266,7 +266,8 @@
     nq = planes * queries
     aw = kin // planes
     grows, gcols = inverse_gram.shape
-    mb, kb = min(512, grows), min(2048, gcols)
+    mb, kb = min(512, grows // subs), min(2048, gcols)
+    per = grows // subs // mb
     examples, width = store_slab.shape
     half = queries // 2
     hq = nq // subs
@@ -278,13 +279,14 @@
         pltpu.VMEM((SLOTS, mb, kb), F32), pltpu.VMEM(store_slab.shape, BF16),
         pltpu.VMEM((queries, 2, tokens, kin), F32), pltpu.VMEM((queries, 2, tokens, kin), F32),
         pltpu.VMEM((half, kin, kout), F32), pltpu.VMEM((planes, queries, aw, kout), F32),
-        pltpu.VMEM((gcols, lanes), BF16), pltpu.VMEM((grows, lanes), F32),
-        pltpu.VMEM((subs, nq, width), F32), pltpu.VMEM((nq, width), F32), pltpu.VMEM((cols, nq, width), F32),
+        pltpu.VMEM((gcols, lanes), BF16),
+        pltpu.VMEM((subs * per, nq, mb), F32), pltpu.VMEM((per, nq, mb), F32),
+        pltpu.VMEM((cols, per, nq, mb), F32),
         pltpu.VMEM((subs, hq, examples), F32), pltpu.VMEM((hq, examples), F32), pltpu.VMEM((hq, examples), F32),
         pltpu.VMEM((rows, hq, examples), F32), pltpu.VMEM((subs, hq, examples), F32),
         dma((5,)), dma((SLOTS,)), dma((queries, 2)), dma((queries, 2)),
         dma((half, planes)), dma((half, planes)), dma((half,)), dma((queries,)), dma((queries,)),
-        dma((2,)), dma((cols,)), dma((cols,)), dma((2,)), dma((rows,)), dma((rows,)), dma((1,)), dma((2,)),
+        dma((per,)), dma((per,)), dma((cols, per)), dma((cols, per)), dma((2,)), dma((rows,)), dma((rows,)), dma((1,)), dma((2,)),
     ]
     return pl.pallas_call(
         functools.partial(kernel, rows, cols, subs),

time: 84.1 us -> 76 us (0.904)
  Pallas kernels: 82.5 us -> 74.4 us
    pallas_call x1, Pallas kernels: 82.5 us -> 74.4 us  [body(): pl.pallas_call(functools.partial(kernel, rows, cols, subs), out_shape=jax...]
where the time goes in v4:
time: 76 us; the launch traced here: 75.9 us
  Pallas kernels  74.4 us (98%)
  local copies, waits for them, and re-layouts  1.47 us (2%)
    pallas_call x1, Pallas kernels, body(): pl.pallas_call(functools.partial(kernel, rows, cols, subs), out_shape=jax...  74.4 us

profile of v4, /device:TPU:0, one launch (start us, length us, event | category | flops | bytes accessed | tf_op | source)
XLA Modules:
  0.0 75.9 jit_solution(14799867233041873752)
XLA Ops:
  0.0 74.4 %influence.1 = f32[32,512]{1,0:T(8,128)} custom-call(bf16[8,128,1024]{2,1,0:T(8,128)(2,1)} %acts_h.1, bf16[8,128,1024]{2,1,0:T(8,128)(2,1)} %grads_h.1, bf16[1024,128]{1,0:T(8,128)(2,1)} %pin_h.1, bf16[1024,128]{1,0:T(8,128)(2,1)} %pout_h.1, f32[4096,4096]{1,0:T(8,128)} %gram_h.1, bf16[512,2048]{1,0:T(8,128)(2,1)} %store_h.1), custom_call_target="tpu_custom_call" | custom-call | tf_op jit(solution)/shard_map/influence/pallas_call | solution.py:291
  74.4 1.5 %copy.8 = f32[32,512]{1,0:T(8,128)} copy(f32[32,512]{1,0:T(8,128)} %influence.1) | data formatting | bytes 131072

commit v5 on v4

--- a/solution.py
+++ b/solution.py
@@ -56,10 +56,6 @@
             gram_h.at[pl.ds(pl.multiple_of(i * mb, mb), mb), pl.ds(pl.multiple_of(k * kb, kb), kb)],
             gram.at[slot], gram_sem.at[slot])
 
-    for b in range(min(SLOTS, blocks)):
-        gram_copy(b).start()
-    loads[4].start()
-
     barrier = pltpu.get_barrier_semaphore()
     count = 0
     for d in range(1, rows):
@@ -76,6 +72,9 @@
 
     for l in loads[:4]:
         l.wait()
+    for b in range(min(SLOTS, blocks)):
+        gram_copy(b).start()
+    loads[4].start()
     for q in range(queries):
         project(q)
     pl.semaphore_wait(barrier, count)

time: 76 us -> 66 us (0.87)
  Pallas kernels: 74.4 us -> 64.4 us
    pallas_call x1, Pallas kernels: 74.4 us -> 64.4 us  [body(): pl.pallas_call(functools.partial(kernel, rows, cols, subs), out_shape=jax...]
where the time goes in v5:
time: 66 us; the launch traced here: 65.8 us
  Pallas kernels  64.4 us (98%)
  local copies, waits for them, and re-layouts  1.47 us (2%)
    pallas_call x1, Pallas kernels, body(): pl.pallas_call(functools.partial(kernel, rows, cols, subs), out_shape=jax...  64.4 us
    unnamed x1, local copies, waits for them, and re-layouts  1.47 us

profile of v5, /device:TPU:0, one launch (start us, length us, event | category | flops | bytes accessed | tf_op | source)
XLA Modules:
  0.0 65.8 jit_solution(12338989482371889737)
XLA Ops:
  0.0 64.4 %influence.1 = f32[32,512]{1,0:T(8,128)} custom-call(bf16[8,128,1024]{2,1,0:T(8,128)(2,1)} %acts_h.1, bf16[8,128,1024]{2,1,0:T(8,128)(2,1)} %grads_h.1, bf16[1024,128]{1,0:T(8,128)(2,1)} %pin_h.1, bf16[1024,128]{1,0:T(8,128)(2,1)} %pout_h.1, f32[4096,4096]{1,0:T(8,128)} %gram_h.1, bf16[512,2048]{1,0:T(8,128)(2,1)} %store_h.1), custom_call_target="tpu_custom_call" | custom-call | tf_op jit(solution)/shard_map/influence/pallas_call | solution.py:290
  64.4 1.5 %copy.8 = f32[32,512]{1,0:T(8,128)} copy(f32[32,512]{1,0:T(8,128)} %influence.1) | data formatting | bytes 131072
